TPU v7x, 768 devices: a whole 4x8x12 slice. The times are simulated.
768 devices in a mesh: energy: 32 (over y, x), atom: 24 (over z, core).
Axes of the slice: x: 4, y: 8, z: 12, core: 2. Of those that a mesh axis runs over, the one named last changes fastest.
Arguments:
- green_ret: bfloat16 [2, 12, 12, 1536, 768], P(None, None, None, ('energy', 'atom')), may hold values from -1.59375 to 1.59375
- broadening: bfloat16 [2, 2, 12, 12, 1536, 768], P(None, None, None, None, ('energy', 'atom')), may hold values from -6 to 6
- coupling: float32 [64], replicated, may hold values from 0.01 to 0.1
- occupation: float32 [64], replicated, may hold values from 0.05 to 3
- shifts: int32 [64], replicated, may hold values from 1 to 2, as said below
- neighbours: int32 [768, 34], P('atom'), may hold values from -24 to 791, as said below
- bond_count: int32 [768], P('atom'), may hold values from 17 to 34
- bond_weight: bfloat16 [768, 34], P('atom'), may hold values from -1 to 1
Outputs:
- self_energy: bfloat16 [2, 2, 12, 12, 1536, 768], P(None, None, None, None, ('energy', 'atom'))
- polarization: float32 [64, 768], P('energy', 'atom')
Inputs may be any that keep to these rules, and one draw needn't show every extreme that they name: `shifts`: each mode's energy in energy steps. `neighbours`: the entries of row a are distinct and lie within 24 of a; entries outside 0 .. 767 name no atom. `bond_count`: the live slots of an atom are the leading ones of its row.
All inputs are finite; a program needn't handle non-finite values.
Results may differ from a plain program's by a relative error of at most 0.0076.
Values may be sent and summed in bfloat16 or wider, within the bound.
No kernel may reach another device: no remote copies, remote signals or barrier semaphores. Data moves between devices by JAX's collectives and lax.ppermute only.
A program may use at most 128 MiB of HBM per device.

v0:
```python
import functools
import math

import jax
import jax.numpy as jnp
from jax import lax
from jax.experimental import pallas as pl
from jax.experimental.pallas import tpu as pltpu
from jax.sharding import PartitionSpec as P

REACH = 24
SHIFT = 2
ORB = 12
TILES = 6
ROWS = 12
BOTH = ("energy", "atom")
F32 = jnp.float32
BF16 = jnp.bfloat16
PRECISE = lax.Precision.HIGHEST


def natural(x):
    lead = x.shape[:-4]
    x = x.reshape(*lead, ORB, ORB, 2, TILES, 128)
    x = jnp.swapaxes(x, -3, -2)
    return x.reshape(*lead, ORB * ORB * ROWS, 128)


def from_natural(x):
    lead = x.shape[:-2]
    x = x.reshape(*lead, ORB, ORB, TILES, 2, 128)
    x = jnp.swapaxes(x, -3, -2)
    return x.reshape(*lead, ORB, ORB, 2, TILES * 128)


def low_half():
    return lax.broadcasted_iota(jnp.int32, (8, 128), 0) < 4


def turned(v):
    return pltpu.roll(v, 4, 0)


def doubled(v0, v1, v2, low):
    r0, r1, r2 = turned(v0), turned(v1), turned(v2)
    first = (v0, jnp.where(low, v1, r0), jnp.where(low, r0, r1))
    second = (jnp.where(low, r1, r2), jnp.where(low, r2, v1), v2)
    return first, second


def keldysh_kernel(first_row, rows, g_ref, b_ref, out_ref, gd, bn, hd, kn):
    low = low_half()

    def prepare(q, carry):
        start = pl.multiple_of(q * 48, 48)
        for c in range(2):
            x = g_ref[c, pl.ds(start, 48), :].astype(F32)
            y = b_ref[0, c, pl.ds(start, 48), :].astype(F32)
            for half in range(2):
                v = [x[24 * half + 8 * m : 24 * half + 8 * m + 8] for m in range(3)]
                for e, copy in enumerate(doubled(*v, low)):
                    for m in range(3):
                        gd[c, (q * 4 + half * 2 + e) * 3 + m] = copy[m]
            for m in range(6):
                bn[c, q * 6 + m] = y[8 * m : 8 * m + 8]
        return carry

    lax.fori_loop(0, 36, prepare, 0)

    def stage_one(step, carry):
        il = step // 3
        jb = step % 3
        re = [[[None] * 3 for _ in range(2)] for _ in range(2)]
        im = [[[None] * 3 for _ in range(2)] for _ in range(2)]
        for k in range(ORB):
            a = [
                [[gd[c, ((first_row + il * 2 + i) * ORB + k) * 3 + m] for m in range(3)] for i in range(2)]
                for c in range(2)
            ]
            b = [
                [[bn[c, (k * 6 + jb * 2 + p) * 3 + m] for m in range(3)] for p in range(2)]
                for c in range(2)
            ]
            for i in range(2):
                for p in range(2):
                    for m in range(3):
                        ar, ai = a[0][i][m], a[1][i][m]
                        br, bi = b[0][p][m], b[1][p][m]
                        if k == 0:
                            re[i][p][m] = ar * br - ai * bi
                            im[i][p][m] = ar * bi + ai * br
                        else:
                            re[i][p][m] = re[i][p][m] + ar * br - ai * bi
                            im[i][p][m] = im[i][p][m] + ar * bi + ai * br
        for i in range(2):
            for p in range(2):
                for c, value in ((0, re), (1, im)):
                    for e, copy in enumerate(doubled(*value[i][p], low)):
                        for m in range(3):
                            hd[c, ((il * 2 + i) * ORB + (jb * 2 + p) * 2 + e) * 3 + m] = copy[m]
        return carry

    lax.fori_loop(0, (rows // 2) * 3, stage_one, 0)

    def stage_two(step, carry):
        il = step // 3
        jb = step % 3
        re = [[[None] * 3 for _ in range(2)] for _ in range(2)]
        im = [[[None] * 3 for _ in range(2)] for _ in range(2)]
        for k in range(ORB):
            a = [
                [[hd[c, ((il * 2 + i) * ORB + k) * 3 + m] for m in range(3)] for i in range(2)]
                for c in range(2)
            ]
            b = []
            for c in range(2):
                pairs = []
                for p in range(2):
                    j0 = ((jb * 4 + p * 2) * ORB + k) * 3
                    j1 = j0 + ORB * 3
                    pairs.append(
                        (gd[c, j0], jnp.where(low, gd[c, j0 + 1], gd[c, j1 + 1]), gd[c, j1 + 2])
                    )
                b.append(pairs)
            for i in range(2):
                for p in range(2):
                    for m in range(3):
                        ar, ai = a[0][i][m], a[1][i][m]
                        br, bi = b[0][p][m], b[1][p][m]
                        if k == 0:
                            re[i][p][m] = ar * br + ai * bi
                            im[i][p][m] = ai * br - ar * bi
                        else:
                            re[i][p][m] = re[i][p][m] + ar * br + ai * bi
                            im[i][p][m] = im[i][p][m] + ai * br - ar * bi
        for i in range(2):
            for p in range(2):
                for c, value in ((0, re), (1, im)):
                    for m in range(3):
                        row = (c * rows * ORB * ROWS) + (
                            ((il * 2 + i) * 6 + jb * 2 + p) * 3 + m
                        ) * 8
                        kn[pl.ds(pl.multiple_of(row, 8), 8), :] = value[i][p][m]
        return carry

    lax.fori_loop(0, (rows // 2) * 3, stage_two, 0)

    count = 2 * rows * ORB
    for te in range(ROWS):
        out_ref[te] = kn[pl.ds(te, count, stride=ROWS), :].astype(BF16)


def keldysh(green, broad, species, first_row, rows):
    count = 2 * rows * ORB
    flops = 2 * 8 * rows * 144 * 1536
    return pl.pallas_call(
        functools.partial(keldysh_kernel, first_row, rows),
        grid=(1,),
        in_specs=[
            pl.BlockSpec((2, 1728, 128), lambda n: (0, 0, 0)),
            pl.BlockSpec((1, 2, 1728, 128), lambda n: (species, 0, 0, 0)),
        ],
        out_specs=pl.BlockSpec((ROWS, count, 128), lambda n: (0, 0, 0)),
        out_shape=jax.ShapeDtypeStruct((ROWS, count, 128), BF16),
        scratch_shapes=[
            pltpu.VMEM((2, 432, 8, 128), F32),
            pltpu.VMEM((2, 216, 8, 128), F32),
            pltpu.VMEM((2, rows * 36, 8, 128), F32),
            pltpu.VMEM((count * ROWS, 128), F32),
        ],
        cost_estimate=pl.CostEstimate(
            flops=flops, bytes_accessed=3 * 884736, transcendentals=0
        ),
        name="keldysh",
    )(green, broad)


def bonds_kernel(table_ref, out_ref, wide):
    lane = lax.broadcasted_iota(jnp.int32, (64, 128), 1)
    for t in range(TILES):
        x = table_ref[pl.ds(64 * t, 64), :].astype(F32)
        for odd in range(2):
            kept = jnp.where((lane >= 64) if odd else (lane < 64), x, 0.0)
            kept = jnp.concatenate([kept, jnp.zeros((64, 256), F32)], axis=1)
            start = 128 - REACH + (1 - 64 if odd else 0)
            kept = pltpu.roll(kept, 0, 1, stride=2, stride_axis=0)
            kept = pltpu.roll(kept, start, 1)
            for w in range(3):
                wide[w, pl.ds(odd, 64, stride=2), :] = kept[:, 128 * w : 128 * w + 128]
        for w in range(3):
            out_ref[t, :, 128 * w : 128 * w + 128] = wide[w].astype(BF16)


def bonds(table):
    return pl.pallas_call(
        bonds_kernel,
        out_shape=jax.ShapeDtypeStruct((TILES, 128, 384), BF16),
        in_specs=[pl.BlockSpec(memory_space=pltpu.VMEM)],
        out_specs=pl.BlockSpec(memory_space=pltpu.VMEM),
        scratch_shapes=[pltpu.VMEM((3, 128, 128), F32)],
        cost_estimate=pl.CostEstimate(flops=10**6, bytes_accessed=10**6, transcendentals=0),
        name="bonds",
    )(table)


def scatter_kernel(rows, *refs):
    c_ref, k_ref, a_ref, b_ref, w_ref = refs[:5]
    out_ref, mixed, back = refs[-3:]
    count = 2 * rows * ORB
    up1, dn1 = c_ref[0], c_ref[1]
    a00, a01, a10, a11 = c_ref[2], c_ref[3], c_ref[4], c_ref[5]
    b00, b01, b10, b11 = c_ref[6], c_ref[7], c_ref[8], c_ref[9]

    for t in range(TILES):
        k0 = k_ref[2 * t].astype(F32)
        k1 = k_ref[2 * t + 1].astype(F32)
        a0 = a_ref[2 * t].astype(F32)
        a1 = a_ref[2 * t + 1].astype(F32)
        b0 = b_ref[2 * t].astype(F32)
        b1 = b_ref[2 * t + 1].astype(F32)
        s0 = up1 * k1 + a00 * a0 + a01 * a1 + b00 * b0 + b01 * b1
        s1 = dn1 * k0 + a10 * a0 + a11 * a1 + b10 * b0 + b11 * b1
        mixed[0:count, 128 * t : 128 * t + 128] = s0.astype(BF16)
        mixed[count : 2 * count, 128 * t : 128 * t + 128] = s1.astype(BF16)
    for t in range(TILES):
        lo = max(0, t - 1)
        hi = min(TILES, t + 2)
        skip = lo - (t - 1)
        x = mixed[:, 128 * lo : 128 * hi]
        w = w_ref[t, :, 128 * skip : 128 * (skip + hi - lo)]
        y = lax.dot_general(x, w, (((1,), (1,)), ((), ())), preferred_element_type=F32)
        back[pl.ds(2 * t, count, stride=ROWS), :] = y[0:count]
        back[pl.ds(2 * t + 1, count, stride=ROWS), :] = y[count : 2 * count]
    half = rows * ORB * ROWS
    out_ref[0, 0] = back[0:half].astype(BF16)
    out_ref[0, 1] = back[half : 2 * half].astype(BF16)


def scattered(coefs, own, even, odd, weights, species, first_row, rows, target):
    count = 2 * rows * ORB
    vmem = pl.BlockSpec(memory_space=pltpu.VMEM)
    whole = pl.BlockSpec((ROWS, count, 128), lambda n: (0, 0, 0))
    operands = [coefs, own, even, odd, weights]
    in_specs = [
        pl.BlockSpec(memory_space=pltpu.SMEM),
        whole,
        whole,
        whole,
        pl.BlockSpec((TILES, 128, 384), lambda n: (0, 0, 0)),
    ]
    aliases = {}
    if target is not None:
        operands.append(target)
        in_specs.append(pl.BlockSpec(memory_space=pl.ANY))
        aliases = {5: 0}
    block = first_row // rows
    return pl.pallas_call(
        functools.partial(scatter_kernel, rows),
        grid=(1,),
        in_specs=in_specs,
        out_specs=pl.BlockSpec(
            (1, 2, rows * ORB * ROWS, 128), lambda n: (species, 0, block, 0)
        ),
        out_shape=jax.ShapeDtypeStruct((2, 2, 1728, 128), BF16),
        scratch_shapes=[
            pltpu.VMEM((2 * count, 768), BF16),
            pltpu.VMEM((count * ROWS, 128), F32),
        ],
        input_output_aliases=aliases,
        cost_estimate=pl.CostEstimate(
            flops=4 * count * 384 * 768, bytes_accessed=4 * count * ROWS * 256, transcendentals=0
        ),
        name="scattered",
    )(*operands)


def trace_kernel(pieces, c_ref, *refs):
    lesser = refs[: len(pieces)]
    greater = refs[len(pieces) : 2 * len(pieces)]
    even = refs[2 * len(pieces) : 3 * len(pieces)]
    odd = refs[3 * len(pieces) : 4 * len(pieces)]
    out_ref, ks, gs, ps = refs[-4:]
    from_even, from_odd = c_ref[10], c_ref[11]

    for t in range(TILES):
        for n, (first_row, rows) in enumerate(pieces):
            span = rows * ORB
            for e in range(2):
                k = lesser[n][2 * t + e].astype(F32)
                g = greater[n][2 * t + e].astype(F32)
                p = from_even * even[n][2 * t + e].astype(F32) + from_odd * odd[n][
                    2 * t + e
                ].astype(F32)
                for c in range(2):
                    at = c * 144 + first_row * ORB
                    ks[e, at : at + span] = k[c * span : c * span + span]
                    gs[e, at : at + span] = g[c * span : c * span + span]
                    ps[e, at : at + span] = p[c * span : c * span + span]
        one = jnp.zeros((ORB, 128), F32)
        two = jnp.zeros((ORB, 128), F32)
        for c in range(2):
            for i in range(ORB):
                at = c * 144 + ORB * i
                k0 = ks[0, pl.ds(at, ORB), :]
                k1 = ks[1, pl.ds(at, ORB), :]
                g0 = gs[0, pl.ds(c * 144 + i, ORB, stride=ORB), :]
                p0 = ps[0, pl.ds(c * 144 + i, ORB, stride=ORB), :]
                p1 = ps[1, pl.ds(c * 144 + i, ORB, stride=ORB), :]
                first = k0 * p1 + k1 * g0
                second = k0 * p0 + k1 * p1
                if c == 0:
                    one, two = one + first, two + second
                else:
                    one, two = one - first, two - second
        out_ref[0, t : t + 1] = jnp.sum(one, axis=0, keepdims=True)
        out_ref[1, t : t + 1] = jnp.sum(two, axis=0, keepdims=True)


def traced(coefs, pieces, lesser, greater, even, odd):
    vmem = pl.BlockSpec(memory_space=pltpu.VMEM)
    return pl.pallas_call(
        functools.partial(trace_kernel, pieces),
        out_shape=jax.ShapeDtypeStruct((2, TILES, 128), F32),
        in_specs=[pl.BlockSpec(memory_space=pltpu.SMEM)] + [vmem] * (4 * len(pieces)),
        out_specs=vmem,
        scratch_shapes=[pltpu.VMEM((2, 288, 128), F32)] * 3,
        cost_estimate=pl.CostEstimate(
            flops=8 * 288 * 1536, bytes_accessed=4 * 884736, transcendentals=0
        ),
        name="traced",
    )(coefs, *lesser, *greater, *even, *odd)


def everyone(x, axis):
    length = lax.axis_size(axis)
    return lax.all_to_all(jnp.broadcast_to(x[None], (length, *x.shape)), axis, 0, 0, tiled=True)


def local(pieces, green_ret, broadening, coupling, occupation, shifts, neighbours, bond_count, bond_weight):
    tile_width = neighbours.shape[0]
    tiles = lax.axis_size("atom")
    devices = tiles * lax.axis_size("energy")
    total_energies = 2 * devices
    green = natural(green_ret)
    broad = natural(broadening)

    active = jnp.arange(neighbours.shape[1], dtype=jnp.int32)[None, :] < bond_count[:, None]
    weights = jnp.where(active, bond_weight.astype(F32), 0.0)
    own_atoms = lax.axis_index("atom") * tile_width + jnp.arange(tile_width, dtype=jnp.int32)
    offset = neighbours - own_atoms[:, None] + REACH
    lanes = jnp.arange(64, dtype=jnp.int32)
    table = jnp.sum(
        jnp.where(offset[:, :, None] == lanes[None, None, :], weights[:, :, None], 0.0), axis=1
    ).astype(BF16)
    tables = everyone(table.reshape(tile_width // 2, 128), "atom")

    levels = jnp.arange(1, SHIFT + 1, dtype=jnp.int32)
    onehot = (shifts[:, None] == levels[None, :]).astype(F32)
    emission = jnp.dot(coupling * (occupation + 1.0), onehot, precision=PRECISE)
    absorption = jnp.dot(coupling * occupation, onehot, precision=PRECISE)
    emission = lax.reduce_precision(emission, 8, 7)
    absorption = lax.reduce_precision(absorption, 8, 7)
    parity = lax.axis_index("atom") % 2
    is_even = parity == 0

    def coefs_of(up, down):
        zero = jnp.zeros((), F32)
        nxt = jnp.stack([up[1], zero, up[0], up[1]])
        prv = jnp.stack([down[1], down[0], zero, down[1]])
        a = jnp.where(is_even, nxt, prv)
        b = jnp.where(is_even, prv, nxt)
        own = jnp.stack([up[0], down[0]])
        pick = jnp.where(is_even, jnp.array([0.0, 1.0], F32), jnp.array([1.0, 0.0], F32))
        return jnp.concatenate([own, a, b, pick, jnp.zeros((4,), F32)])

    coefs = (coefs_of(emission, absorption), coefs_of(absorption, emission))

    swap_even = [(i, i ^ 1) for i in range(devices)]
    swap_odd = [(i, i + 1) for i in range(1, devices - 1, 2)]
    swap_odd = swap_odd + [(target, source) for source, target in swap_odd]

    own = {}
    even = {}
    odd = {}
    for species in (1, 0):
        for piece in pieces:
            key = (species, piece)
            own[key] = keldysh(green, broad, species, *piece)
            odd[key] = lax.ppermute(own[key], BOTH, swap_odd)
            even[key] = lax.ppermute(own[key], BOTH, swap_even)
    weights_band = bonds(tables.reshape(tiles * tile_width // 2, 128))

    traces = traced(
        coefs[1],
        pieces,
        [own[0, piece] for piece in pieces],
        [own[1, piece] for piece in pieces],
        [even[1, piece] for piece in pieces],
        [odd[1, piece] for piece in pieces],
    )
    shares = traces.reshape(2, tiles, tile_width)
    shares = jnp.swapaxes(shares, 0, 1).reshape(tiles, 1, 2 * tile_width)
    shares = lax.all_to_all(shares, "atom", 0, 0, tiled=True).sum(axis=0)
    total = everyone(shares, "energy").sum(axis=0).reshape(2, tile_width)
    share_rows = shifts.shape[0] // lax.axis_size("energy")
    first = lax.axis_index("energy") * share_rows
    own_onehot = lax.dynamic_slice_in_dim(onehot, first, share_rows, 0)
    own_coupling = lax.dynamic_slice_in_dim(coupling, first, share_rows, 0)
    picked = own_onehot[:, 0:1] * total[0:1] + own_onehot[:, 1:2] * total[1:2]
    polarization = own_coupling[:, None] * picked / math.sqrt(total_energies)

    result = None
    for species in (1, 0):
        for piece in pieces:
            key = (species, piece)
            result = scattered(
                coefs[species], own[key], even[key], odd[key], weights_band, species, *piece, result
            )
    return (from_natural(result), polarization)


def solution(mesh):
    in_specs = (
        P(None, None, None, ("energy", "atom"), None),
        P(None, None, None, None, ("energy", "atom"), None),
        P(),
        P(),
        P(),
        P("atom", None),
        P("atom"),
        P("atom", None),
    )
    out_specs = (P(None, None, None, None, ("energy", "atom"), None), P("energy", "atom"))
    pieces = ((0, 12),)
    return jax.shard_map(
        functools.partial(local, pieces), mesh=mesh, in_specs=in_specs, out_specs=out_specs, check_vma=False
    )
```

profile of v0, /device:TPU:1, one launch (start us, length us, event | category | flops | bytes accessed | tf_op | source)
XLA Modules:
  0.0 130.0 jit_solution(18090010486653675738)
XLA Ops:
  0.6 4.4 %reshape.61 = bf16[2,2,12,12,2,6,128]{6,5,4,3,2,1,0:T(8,128)(2,1)S(1)} reshape(bf16[2,2,12,12,2,768]{5,4,3,2,1,0:T(2,128)(2,1)} %param.13) | data formatting | bytes 3538944 | tf_op jit(solution)/shard_map/reshape | solution.py:24
  5.1 0.0 copy-start.2
  5.1 3.0 %copy.35 = bf16[2,2,12,12,6,2,128]{6,5,4,3,2,1,0:T(2,128)(2,1)} copy(bf16[2,2,12,12,6,2,128]{6,4,5,3,2,1,0:T(8,128)(2,1)S(1)} %bitcast.39) | data formatting | bytes 3538944 | tf_op jit(solution)/shard_map/transpose | solution.py:25
  8.1 0.6 reshape.59
  8.7 1.9 %copy.34 = bf16[2,12,12,6,2,128]{5,4,3,2,1,0:T(2,128)(2,1)} copy(bf16[2,12,12,6,2,128]{5,3,4,2,1,0:T(8,128)(2,1)S(1)} %bitcast.42) | data formatting | bytes 1769472 | tf_op jit(solution)/shard_map/transpose | solution.py:25
  10.6 10.5 %keldysh.3.refs_1_ = bf16[12,288,128]{2,1,0:T(8,128)(2,1)} custom-call(bf16[2,1728,128]{2,1,0:T(8,128)(2,1)} %bitcast.40, bf16[2,2,1728,128]{3,2,1,0:T(8,128)(2,1)} %bitcast.35), custom_call_target="tpu_custom_call" | custom-call | flops 42467328 | bytes 2654208 | tf_op jit(solution)/shard_map/keldysh/pallas_call | solution.py:156
  21.1 12.4 %collective-permute-start.2 = (bf16[12,288,128]{2,1,0:T(8,128)(2,1)}, bf16[12,288,128]{2,1,0:T(8,128)(2,1)S(1)}, u32[]{:S(2)}, u32[]{:S(2)}) collective-permute-start(bf16[12,288,128]{2,1,0:T(8,128)(2,1)} %keldysh.3.refs_1_), channel_id=1, source_target_pairs={{0,1},{1,0},{2,3},{3,2},{4,5},{5,4},{6,7},{7,6},{8,9},{9,8},{10,11... | collective-permute-start | bytes 2654216 | tf_op jit(solution)/shard_map/ppermute | solution.py:390
  33.5 1.9 %collective-permute-start.3 = (bf16[12,288,128]{2,1,0:T(8,128)(2,1)}, bf16[12,288,128]{2,1,0:T(8,128)(2,1)S(1)}, u32[]{:S(2)}, u32[]{:S(2)}) collective-permute-start(bf16[12,288,128]{2,1,0:T(8,128)(2,1)} %keldysh.3.refs_1_), channel_id=1, source_target_pairs={{1,2},{3,4},{5,6},{7,8},{9,10},{11,12},{13,14},{15,16},{17,18},{19... | collective-permute-start | bytes 2654216 | tf_op jit(solution)/shard_map/ppermute | solution.py:389
  35.4 10.5 %keldysh.2.refs_1_.refs_0_ = bf16[12,288,128]{2,1,0:T(8,128)(2,1)} custom-call(bf16[2,1728,128]{2,1,0:T(8,128)(2,1)} %bitcast.41, bf16[2,2,1728,128]{3,2,1,0:T(8,128)(2,1)} %bitcast.36), custom_call_target="tpu_custom_call" | custom-call | flops 42467328 | bytes 2654208 | tf_op jit(solution)/shard_map/keldysh/pallas_call | solution.py:156
  45.9 1.9 %collective-permute-start = (bf16[12,288,128]{2,1,0:T(8,128)(2,1)}, bf16[12,288,128]{2,1,0:T(8,128)(2,1)S(1)}, u32[]{:S(2)}, u32[]{:S(2)}) collective-permute-start(bf16[12,288,128]{2,1,0:T(8,128)(2,1)} %keldysh.2.refs_1_.refs_0_), channel_id=1, source_target_pairs={{0,1},{1,0},{2,3},{3,2},{4,5},{5,4},{6,7},{7,6},{8,9},{9,8},{10,11... | collective-permute-start | bytes 2654216 | tf_op jit(solution)/shard_map/ppermute | solution.py:390
  47.8 3.6 %collective-permute-start.1 = (bf16[12,288,128]{2,1,0:T(8,128)(2,1)}, bf16[12,288,128]{2,1,0:T(8,128)(2,1)S(1)}, u32[]{:S(2)}, u32[]{:S(2)}) collective-permute-start(bf16[12,288,128]{2,1,0:T(8,128)(2,1)} %keldysh.2.refs_1_.refs_0_), channel_id=1, source_target_pairs={{1,2},{3,4},{5,6},{7,8},{9,10},{11,12},{13,14},{15,16},{17,18},{19... | collective-permute-start | bytes 2654216 | tf_op jit(solution)/shard_map/ppermute | solution.py:389
  51.5 0.8 subtract_add_fusion
  52.3 0.7 copy.36
  53.0 0.8 convert_select_fusion
  53.7 0.7 copy.37
  54.4 1.1 select_reduce_fusion
  55.5 0.1 convert_element_type.18
  55.6 0.7 broadcast_in_dim.23
  56.3 7.6 %all-to-all-start = ((bf16[24,16,128]{2,1,0:T(8,128)(2,1)}), bf16[24,16,128]{2,1,0:T(8,128)(2,1)}, u32[]{:S(2)}, u32[]{:S(2)}) async-start(bf16[24,16,128]{2,1,0:T(8,128)(2,1)} %broadcast_in_dim.23), calls=%async_computation | async-start | bytes 196608 | tf_op jit(solution)/shard_map/all_to_all | solution.py:336
  63.9 0.9 fusion
  64.8 0.9 fusion.1
  65.6 1.3 %dynamic_slice.6 = f32[2]{0:T(128)} dynamic-slice(f32[64]{0:T(128)} %param.14, s32[]{:T(128)S(6)} %select_n.62), dynamic_slice_sizes={2} | dynamic-slice | bytes 20 | tf_op jit(solution)/shard_map/dynamic_slice | solution.py:408
  67.0 0.6 fusion.15
  67.5 2.4 %broadcast_select_fusion.1 = (f32[4]{0:T(128)S(1)}, f32[4]{0:T(128)}) fusion(pred[]{:T(512)S(6)} %eq.34, f32[2]{0:T(128)S(1)} %fusion.1, f32[1]{0:T(128)} %constant.11.clone.1, f32[1]{0:T(128)} %get-tuple-element.10, f32[1]{0:T(128)} %get-tuple-element.15, f32[1]{0:T(128)} %get-tuple-element.14), kind=kLoop, calls=%fused_computation.15 | loop fusion | flops 28 | bytes 57 | tf_op jit(solution)/shard_map/jit(_where)/select_n | solution.py:371
  70.0 0.7 broadcast_select_fusion
  70.7 2.5 %concatenate.7.refs_0_.c_ref = f32[16]{0:T(128)} concatenate(f32[1]{0:T(128)} %get-tuple-element.11, f32[1]{0:T(128)} %get-tuple-element.14, f32[4]{0:T(128)} %get-tuple-element.7, f32[4]{0:T(128)S(1)} %get-tuple-element.6, f32[2]{0:T(128)S(1)} %broadcast_select_fusion, f32[4]{0:T(128)S(1)} %broadcast.24), dimensions={0} | concatenate | bytes 128 | tf_op jit(solution)/shard_map/concatenate | solution.py:374
  73.1 2.4 %broadcast_select_fusion.3 = (f32[4]{0:T(128)S(1)}, f32[4]{0:T(128)}) fusion(pred[]{:T(512)S(6)} %eq.34, f32[2]{0:T(128)S(1)} %fusion, f32[1]{0:T(128)} %constant.11.clone.1, f32[1]{0:T(128)} %get-tuple-element.15, f32[1]{0:T(128)} %get-tuple-element.10, f32[1]{0:T(128)} %get-tuple-element.11), kind=kLoop, calls=%fused_computation.17 | loop fusion | flops 28 | bytes 57 | tf_op jit(solution)/shard_map/jit(_where)/select_n | solution.py:371
  75.6 2.5 %concatenate.6.refs_0_ = f32[16]{0:T(128)} concatenate(f32[1]{0:T(128)} %get-tuple-element.14, f32[1]{0:T(128)} %get-tuple-element.11, f32[4]{0:T(128)} %get-tuple-element.9, f32[4]{0:T(128)S(1)} %get-tuple-element.8, f32[2]{0:T(128)S(1)} %broadcast_select_fusion, f32[4]{0:T(128)S(1)} %broadcast.24), dimensions={0} | concatenate | bytes 128 | tf_op jit(solution)/shard_map/concatenate | solution.py:374
  78.0 0.7 compare_convert_fusion
  78.8 0.1 constant_dynamic-slice_fusion
  78.9 2.3 %bonds.1.refs_4_ = bf16[6,128,384]{2,1,0:T(8,128)(2,1)} custom-call(bf16[384,128]{1,0:T(8,128)(2,1)} %bitcast.8.table_ref), custom_call_target="tpu_custom_call" | custom-call | flops 1000000 | bytes 1000000 | tf_op jit(solution)/shard_map/bonds/pallas_call | solution.py:195
  81.1 0.9 copy-done
  82.1 0.9 copy-done.1
  83.0 3.4 %traced.1 = f32[2,6,128]{2,1,0:T(8,128)} custom-call(f32[16]{0:T(128)} %concatenate.7.refs_0_.c_ref, bf16[12,288,128]{2,1,0:T(8,128)(2,1)} %keldysh.2.refs_1_.refs_0_, bf16[12,288,128]{2,1,0:T(8,128)(2,1)} %keldysh.3.refs_1_, bf16[12,288,128]{2,1,0:T(8,128)(2,1)} %copy-done, bf16[12,288,128]{2,1,0:T(8,128)(2,1)} %copy-done.1), custom_call_target="tpu_custom_call" | custom-call | flops 3538944 | bytes 3538944 | tf_op jit(solution)/shard_map/traced/pallas_call | solution.py:321
  86.3 0.8 reshape.66
  87.1 0.7 reshape.67
  87.8 9.4 %all-to-all-start.1 = ((f32[24,1,64]{2,1,0:T(1,128)}), f32[24,1,64]{2,1,0:T(1,128)S(1)}, u32[]{:S(2)}, u32[]{:S(2)}) async-start(f32[24,1,64]{2,1,0:T(1,128)} %bitcast.13), calls=%async_computation.1 | async-start | bytes 24576 | tf_op jit(solution)/shard_map/all_to_all | solution.py:403
  97.2 4.3 %scattered.2.refs_5_ = bf16[2,2,1728,128]{3,2,1,0:T(8,128)(2,1)} custom-call(f32[16]{0:T(128)} %concatenate.7.refs_0_.c_ref, bf16[12,288,128]{2,1,0:T(8,128)(2,1)} %keldysh.3.refs_1_, bf16[12,288,128]{2,1,0:T(8,128)(2,1)} %copy-done, bf16[12,288,128]{2,1,0:T(8,128)(2,1)} %copy-done.1, bf16[6,128,384]{2,1,0:T(8,128)(2,1)} %bonds.1.refs_4_), custom_call_target="tpu_custom_call" | custom-call | flops 339738624 | bytes 3538944 | tf_op jit(solution)/shard_map/scattered/pallas_call | solution.py:257
  101.6 5.1 %all-to-all-done.1 = f32[24,1,64]{2,1,0:T(1,128)S(1)} async-done(((f32[24,1,64]{2,1,0:T(1,128)}), f32[24,1,64]{2,1,0:T(1,128)S(1)}, u32[]{:S(2)}, u32[]{:S(2)}) %all-to-all-start.1) | async-done | bytes 6176 | tf_op jit(solution)/shard_map/all_to_all | solution.py:403
  106.7 0.6 broadcast_in_dim.24
  107.3 11.2 %all-to-all-start.2 = ((f32[32,1,64]{2,1,0:T(1,128)}), f32[32,1,64]{2,1,0:T(1,128)S(1)}, u32[]{:S(2)}, u32[]{:S(2)}) async-start(f32[32,1,64]{2,1,0:T(1,128)} %broadcast_in_dim.24), calls=%async_computation.2 | async-start | bytes 32768 | tf_op jit(solution)/shard_map/all_to_all | solution.py:336
  118.6 0.9 copy-done.3
  119.5 0.9 copy-done.4
  120.5 4.3 %scattered.3 = bf16[2,2,1728,128]{3,2,1,0:T(8,128)(2,1)} custom-call(f32[16]{0:T(128)} %concatenate.6.refs_0_, bf16[12,288,128]{2,1,0:T(8,128)(2,1)} %keldysh.2.refs_1_.refs_0_, bf16[12,288,128]{2,1,0:T(8,128)(2,1)} %copy-done.3, bf16[12,288,128]{2,1,0:T(8,128)(2,1)} %copy-done.4, ...), custom_call_target="tpu_custom_call", output_to_operand_aliasing={{}: (5, {})} | custom-call | flops 339738624 | bytes 3538944 | tf_op jit(solution)/shard_map/scattered/pallas_call | solution.py:257
  124.8 2.1 %copy.43 = bf16[2,2,12,12,6,2,128]{6,4,5,3,2,1,0:T(8,128)(2,1)S(1)} copy(bf16[2,2,12,12,6,2,128]{6,5,4,3,2,1,0:T(2,128)(2,1)} %bitcast.37) | data formatting | bytes 3538944 | tf_op jit(solution)/shard_map/reshape | solution.py:31
  127.0 2.3 %reshape.65 = bf16[2,2,12,12,2,768]{5,4,3,2,1,0:T(2,128)(2,1)} reshape(bf16[2,2,12,12,2,6,128]{6,5,4,3,2,1,0:T(8,128)(2,1)S(1)} %bitcast.38) | data formatting | bytes 3538944 | tf_op jit(solution)/shard_map/reshape | solution.py:33
  129.3 0.1 slice_bitcast_fusion.2
  129.3 0.6 multiply_multiply_fusion
  (22 shorter events, 0.1 us)
Async XLA Ops:
  5.1 3.0 %copy-start.2 = (bf16[2,12,12,2,768]{4,3,2,1,0:T(2,128)(2,1)S(1)}, bf16[2,12,12,2,768]{4,3,2,1,0:T(2,128)(2,1)}, u32[]{:S(2)}) copy-start(bf16[2,12,12,2,768]{4,3,2,1,0:T(2,128)(2,1)} %param.12) | copy-start | bytes 2654212
  21.1 60.0 %collective-permute-start.2 = (bf16[12,288,128]{2,1,0:T(8,128)(2,1)}, bf16[12,288,128]{2,1,0:T(8,128)(2,1)S(1)}, u32[]{:S(2)}, u32[]{:S(2)}) collective-permute-start(bf16[12,288,128]{2,1,0:T(8,128)(2,1)} %keldysh.3.refs_1_), channel_id=1, source_target_pairs={{0,1},{1,0},{2,3},{3,2},{4,5},{5,4},{6,7},{7,6},{8,9},{9,8},{10,11... | collective-permute-start | bytes 2654216 | tf_op jit(solution)/shard_map/ppermute | solution.py:390
  33.5 47.6 %collective-permute-start.3 = (bf16[12,288,128]{2,1,0:T(8,128)(2,1)}, bf16[12,288,128]{2,1,0:T(8,128)(2,1)S(1)}, u32[]{:S(2)}, u32[]{:S(2)}) collective-permute-start(bf16[12,288,128]{2,1,0:T(8,128)(2,1)} %keldysh.3.refs_1_), channel_id=1, source_target_pairs={{1,2},{3,4},{5,6},{7,8},{9,10},{11,12},{13,14},{15,16},{17,18},{19... | collective-permute-start | bytes 2654216 | tf_op jit(solution)/shard_map/ppermute | solution.py:389
  45.9 72.6 %collective-permute-start = (bf16[12,288,128]{2,1,0:T(8,128)(2,1)}, bf16[12,288,128]{2,1,0:T(8,128)(2,1)S(1)}, u32[]{:S(2)}, u32[]{:S(2)}) collective-permute-start(bf16[12,288,128]{2,1,0:T(8,128)(2,1)} %keldysh.2.refs_1_.refs_0_), channel_id=1, source_target_pairs={{0,1},{1,0},{2,3},{3,2},{4,5},{5,4},{6,7},{7,6},{8,9},{9,8},{10,11... | collective-permute-start | bytes 2654216 | tf_op jit(solution)/shard_map/ppermute | solution.py:390
  47.8 70.8 %collective-permute-start.1 = (bf16[12,288,128]{2,1,0:T(8,128)(2,1)}, bf16[12,288,128]{2,1,0:T(8,128)(2,1)S(1)}, u32[]{:S(2)}, u32[]{:S(2)}) collective-permute-start(bf16[12,288,128]{2,1,0:T(8,128)(2,1)} %keldysh.2.refs_1_.refs_0_), channel_id=1, source_target_pairs={{1,2},{3,4},{5,6},{7,8},{9,10},{11,12},{13,14},{15,16},{17,18},{19... | collective-permute-start | bytes 2654216 | tf_op jit(solution)/shard_map/ppermute | solution.py:389
  56.3 22.6 %all-to-all-start = ((bf16[24,16,128]{2,1,0:T(8,128)(2,1)}), bf16[24,16,128]{2,1,0:T(8,128)(2,1)}, u32[]{:S(2)}, u32[]{:S(2)}) async-start(bf16[24,16,128]{2,1,0:T(8,128)(2,1)} %broadcast_in_dim.23), calls=%async_computation | async-start | bytes 196608 | tf_op jit(solution)/shard_map/all_to_all | solution.py:336
  63.9 0.9 copy-start.6
  81.1 0.9 copy-start
  82.1 0.9 copy-start.1
  87.8 18.9 %all-to-all-start.1 = ((f32[24,1,64]{2,1,0:T(1,128)}), f32[24,1,64]{2,1,0:T(1,128)S(1)}, u32[]{:S(2)}, u32[]{:S(2)}) async-start(f32[24,1,64]{2,1,0:T(1,128)} %bitcast.13), calls=%async_computation.1 | async-start | bytes 24576 | tf_op jit(solution)/shard_map/all_to_all | solution.py:403
  107.3 21.9 %all-to-all-start.2 = ((f32[32,1,64]{2,1,0:T(1,128)}), f32[32,1,64]{2,1,0:T(1,128)S(1)}, u32[]{:S(2)}, u32[]{:S(2)}) async-start(f32[32,1,64]{2,1,0:T(1,128)} %broadcast_in_dim.24), calls=%async_computation.2 | async-start | bytes 32768 | tf_op jit(solution)/shard_map/all_to_all | solution.py:336
  118.6 1.0 copy-start.3
  119.5 0.9 copy-start.4
  126.9 2.4 %copy-start.5 = (f32[2]{0:T(128)S(1)}, f32[2]{0:T(128)}, u32[]{:S(2)}) copy-start(f32[2]{0:T(128)} %dynamic_slice.6) | copy-start | bytes 28
where the time goes:
time: 131 us; the launch traced here: 130 us
  starting transfers between devices  48 us (37%)
  Pallas kernels  35.3 us (27%)
  local copies, waits for them, and re-layouts  29.3 us (22%)
  other arithmetic  9.64 us (7%)
  waiting for transfers between devices  5.11 us (4%)
  matrix products  1.76 us (1%)
    pallas_call x2, Pallas kernels, keldysh(): pl.pallas_call(functools.partial(keldysh_kernel, first_row, rows), grid=(...  21 us
    all_to_all x2, starting transfers between devices, everyone(): lax.all_to_all(jnp.broadcast_to(x[None], (length, *x.shape)), axis, 0, 0,...  18.8 us
    ppermute x2, starting transfers between devices, local(): even[key] = lax.ppermute(own[key], BOTH, swap_even)  14.3 us
    all_to_all x1, starting transfers between devices, local(): shares = lax.all_to_all(shares, 'atom', 0, 0, tiled=True).sum(axis=0)  9.41 us
    pallas_call x2, Pallas kernels, scattered(): pl.pallas_call(functools.partial(scatter_kernel, rows), grid=(1,), in_spe...  8.69 us
    ppermute x2, starting transfers between devices, local(): odd[key] = lax.ppermute(own[key], BOTH, swap_odd)  5.56 us
    all_to_all x1, waiting for transfers between devices, local(): shares = lax.all_to_all(shares, 'atom', 0, 0, tiled=True).sum(axis=0)  5.1 us
    reshape x2, local copies, waits for them, and re-layouts, natural(): x = x.reshape(*lead, ORB, ORB, 2, TILES, 128)  5.03 us
  transfers between devices with their start and end apart: 7, of which 1 were waited for; matrix products, arithmetic and copies ran while one was open for 20% of the time, Pallas kernels for 19%

commit v1 on v0

--- a/solution.py
+++ b/solution.py
@@ -5,6 +5,7 @@
 import jax.numpy as jnp
 from jax import lax
 from jax.experimental import pallas as pl
+from jax.experimental.layout import Layout, with_layout_constraint
 from jax.experimental.pallas import tpu as pltpu
 from jax.sharding import PartitionSpec as P
 
@@ -22,14 +23,22 @@
 def natural(x):
     lead = x.shape[:-4]
     x = x.reshape(*lead, ORB, ORB, 2, TILES, 128)
+    n = x.ndim
+    order = tuple(range(n - 3)) + (n - 2, n - 3, n - 1)
+    x = with_layout_constraint(x, Layout(major_to_minor=order))
     x = jnp.swapaxes(x, -3, -2)
+    x = with_layout_constraint(x, Layout(major_to_minor=tuple(range(n))))
     return x.reshape(*lead, ORB * ORB * ROWS, 128)
 
 
 def from_natural(x):
     lead = x.shape[:-2]
     x = x.reshape(*lead, ORB, ORB, TILES, 2, 128)
+    n = x.ndim
+    x = with_layout_constraint(x, Layout(major_to_minor=tuple(range(n))))
     x = jnp.swapaxes(x, -3, -2)
+    order = tuple(range(n - 3)) + (n - 2, n - 3, n - 1)
+    x = with_layout_constraint(x, Layout(major_to_minor=order))
     return x.reshape(*lead, ORB, ORB, 2, TILES * 128)
 
 
@@ -356,22 +365,29 @@
 
     levels = jnp.arange(1, SHIFT + 1, dtype=jnp.int32)
     onehot = (shifts[:, None] == levels[None, :]).astype(F32)
-    emission = jnp.dot(coupling * (occupation + 1.0), onehot, precision=PRECISE)
-    absorption = jnp.dot(coupling * occupation, onehot, precision=PRECISE)
-    emission = lax.reduce_precision(emission, 8, 7)
-    absorption = lax.reduce_precision(absorption, 8, 7)
-    parity = lax.axis_index("atom") % 2
-    is_even = parity == 0
+    emit = coupling * (occupation + 1.0)
+    absorb = coupling * occupation
+    emission = lax.reduce_precision(jnp.sum(emit[:, None] * onehot, axis=0), 8, 7)
+    absorption = lax.reduce_precision(jnp.sum(absorb[:, None] * onehot, axis=0), 8, 7)
+    is_even = lax.axis_index("atom") % 2 == 0
+    slot = jnp.arange(16, dtype=jnp.int32)
 
     def coefs_of(up, down):
-        zero = jnp.zeros((), F32)
-        nxt = jnp.stack([up[1], zero, up[0], up[1]])
-        prv = jnp.stack([down[1], down[0], zero, down[1]])
-        a = jnp.where(is_even, nxt, prv)
-        b = jnp.where(is_even, prv, nxt)
-        own = jnp.stack([up[0], down[0]])
-        pick = jnp.where(is_even, jnp.array([0.0, 1.0], F32), jnp.array([1.0, 0.0], F32))
-        return jnp.concatenate([own, a, b, pick, jnp.zeros((4,), F32)])
+        def at(*places):
+            found = slot == places[0]
+            for place in places[1:]:
+                found = found | (slot == place)
+            return found
+
+        def either(even_places, odd_places):
+            return jnp.where(is_even, at(*even_places), at(*odd_places))
+
+        value = jnp.zeros((16,), F32)
+        value = jnp.where(either((0, 4), (0, 8)), up[0], value)
+        value = jnp.where(either((2, 5), (6, 9)), up[1], value)
+        value = jnp.where(either((1, 7), (1, 3)), down[0], value)
+        value = jnp.where(either((6, 9), (2, 5)), down[1], value)
+        return jnp.where(either((11,), (10,)), 1.0, value)
 
     coefs = (coefs_of(emission, absorption), coefs_of(absorption, emission))
 

time: 131 us -> 111 us (0.85)
  local copies, waits for them, and re-layouts: 29.3 us -> 8.69 us
  waiting for transfers between devices: 5.11 us -> 11.6 us
  starting transfers between devices: 48 us -> 44.7 us
  matrix products: 1.76 us -> 0 us
    reshape x4 -> x0, local copies, waits for them, and re-layouts: 9.44 us -> none  [the longest x2 5.03 us: natural(): x = x.reshape(*lead, ORB, ORB, 2, TILES, 128)]
    all_to_all x2, waiting for transfers between devices: 0.01 us -> 6.52 us  [everyone(): lax.all_to_all(jnp.broadcast_to(x[None], (length, *x.shape)), axis, 0, 0,...]
    concatenate x2 -> x0, local copies, waits for them, and re-layouts: 4.95 us -> none  [coefs_of(): return jnp.concatenate([own, a, b, pick, jnp.zeros((4,), F32)])]
    transpose x2 -> x0, local copies, waits for them, and re-layouts: 4.88 us -> none  [natural(): x = jnp.swapaxes(x, -3, -2)]
    all_to_all x1, starting transfers between devices: 9.41 us -> 6.02 us  [local(): shares = lax.all_to_all(shares, 'atom', 0, 0, tiled=True).sum(axis=0)]
    select_n x3 -> x1, other arithmetic: 5.55 us -> 3.1 us  [coefs_of(): return jnp.where(either((11,), (10,)), 1.0, value)]
    dot_general x2 -> x0, matrix products: 1.76 us -> none  [the longest x1 0.88 us: local(): absorption = jnp.dot(coupling * occupation, onehot, precision=PRECISE)]
    unnamed x14 -> x8, local copies, waits for them, and re-layouts: 3.74 us -> 2.41 us
  transfers between devices with their start and end apart: 7 -> 7, of which waited for: 1 -> 3; matrix products, arithmetic and copies ran while one was open for 20% -> 13% of each run, Pallas kernels for 19% -> 23%
where the time goes in v1:
time: 111 us; the launch traced here: 110 us
  starting transfers between devices  44.7 us (40%)
  Pallas kernels  35.3 us (32%)
  waiting for transfers between devices  11.6 us (10%)
  other arithmetic  8.74 us (8%)
  local copies, waits for them, and re-layouts  8.69 us (8%)
    pallas_call x2, Pallas kernels, keldysh(): pl.pallas_call(functools.partial(keldysh_kernel, first_row, rows), grid=(...  21 us
    all_to_all x2, starting transfers between devices, everyone(): lax.all_to_all(jnp.broadcast_to(x[None], (length, *x.shape)), axis, 0, 0,...  18.8 us
    ppermute x2, starting transfers between devices, local(): even[key] = lax.ppermute(own[key], BOTH, swap_even)  14.3 us
    pallas_call x2, Pallas kernels, scattered(): pl.pallas_call(functools.partial(scatter_kernel, rows), grid=(1,), in_spe...  8.69 us
    all_to_all x2, waiting for transfers between devices, everyone(): lax.all_to_all(jnp.broadcast_to(x[None], (length, *x.shape)), axis, 0, 0,...  6.52 us
    all_to_all x1, starting transfers between devices, local(): shares = lax.all_to_all(shares, 'atom', 0, 0, tiled=True).sum(axis=0)  6.02 us
    ppermute x2, starting transfers between devices, local(): odd[key] = lax.ppermute(own[key], BOTH, swap_odd)  5.56 us
    all_to_all x1, waiting for transfers between devices, local(): shares = lax.all_to_all(shares, 'atom', 0, 0, tiled=True).sum(axis=0)  5.1 us
  transfers between devices with their start and end apart: 7, of which 3 were waited for; matrix products, arithmetic and copies ran while one was open for 13% of the time, Pallas kernels for 23%

profile of v1, /device:TPU:1, one launch (start us, length us, event | category | flops | bytes accessed | tf_op | source)
XLA Modules:
  0.0 109.9 jit_solution(5235752209603204348)
XLA Ops:
  0.6 10.5 %keldysh.3.refs_1_ = bf16[12,288,128]{2,1,0:T(8,128)(2,1)} custom-call(bf16[2,1728,128]{2,1,0:T(8,128)(2,1)} %bitcast.35, bf16[2,2,1728,128]{3,2,1,0:T(8,128)(2,1)} %bitcast.32), custom_call_target="tpu_custom_call" | custom-call | flops 42467328 | bytes 2654208 | tf_op jit(solution)/shard_map/keldysh/pallas_call | solution.py:165
  11.2 12.4 %collective-permute-start.2 = (bf16[12,288,128]{2,1,0:T(8,128)(2,1)}, bf16[12,288,128]{2,1,0:T(8,128)(2,1)S(1)}, u32[]{:S(2)}, u32[]{:S(2)}) collective-permute-start(bf16[12,288,128]{2,1,0:T(8,128)(2,1)} %keldysh.3.refs_1_), channel_id=1, source_target_pairs={{0,1},{1,0},{2,3},{3,2},{4,5},{5,4},{6,7},{7,6},{8,9},{9,8},{10,11... | collective-permute-start | bytes 2654216 | tf_op jit(solution)/shard_map/ppermute | solution.py:406
  23.5 1.9 %collective-permute-start.3 = (bf16[12,288,128]{2,1,0:T(8,128)(2,1)}, bf16[12,288,128]{2,1,0:T(8,128)(2,1)S(1)}, u32[]{:S(2)}, u32[]{:S(2)}) collective-permute-start(bf16[12,288,128]{2,1,0:T(8,128)(2,1)} %keldysh.3.refs_1_), channel_id=1, source_target_pairs={{1,2},{3,4},{5,6},{7,8},{9,10},{11,12},{13,14},{15,16},{17,18},{19... | collective-permute-start | bytes 2654216 | tf_op jit(solution)/shard_map/ppermute | solution.py:405
  25.5 10.5 %keldysh.2.refs_1_.refs_0_ = bf16[12,288,128]{2,1,0:T(8,128)(2,1)} custom-call(bf16[2,1728,128]{2,1,0:T(8,128)(2,1)} %bitcast.36, bf16[2,2,1728,128]{3,2,1,0:T(8,128)(2,1)} %bitcast.33), custom_call_target="tpu_custom_call" | custom-call | flops 42467328 | bytes 2654208 | tf_op jit(solution)/shard_map/keldysh/pallas_call | solution.py:165
  36.0 1.9 %collective-permute-start = (bf16[12,288,128]{2,1,0:T(8,128)(2,1)}, bf16[12,288,128]{2,1,0:T(8,128)(2,1)S(1)}, u32[]{:S(2)}, u32[]{:S(2)}) collective-permute-start(bf16[12,288,128]{2,1,0:T(8,128)(2,1)} %keldysh.2.refs_1_.refs_0_), channel_id=1, source_target_pairs={{0,1},{1,0},{2,3},{3,2},{4,5},{5,4},{6,7},{7,6},{8,9},{9,8},{10,11... | collective-permute-start | bytes 2654216 | tf_op jit(solution)/shard_map/ppermute | solution.py:406
  37.9 3.6 %collective-permute-start.1 = (bf16[12,288,128]{2,1,0:T(8,128)(2,1)}, bf16[12,288,128]{2,1,0:T(8,128)(2,1)S(1)}, u32[]{:S(2)}, u32[]{:S(2)}) collective-permute-start(bf16[12,288,128]{2,1,0:T(8,128)(2,1)} %keldysh.2.refs_1_.refs_0_), channel_id=1, source_target_pairs={{1,2},{3,4},{5,6},{7,8},{9,10},{11,12},{13,14},{15,16},{17,18},{19... | collective-permute-start | bytes 2654216 | tf_op jit(solution)/shard_map/ppermute | solution.py:405
  41.5 0.8 subtract_add_fusion
  42.3 0.7 copy.18
  43.0 0.8 convert_select_fusion
  43.8 0.7 copy.19
  44.5 1.1 select_reduce_fusion
  45.6 0.1 convert_element_type.18
  45.7 0.7 broadcast_in_dim.68
  46.3 7.6 %all-to-all-start = ((bf16[24,16,128]{2,1,0:T(8,128)(2,1)}), bf16[24,16,128]{2,1,0:T(8,128)(2,1)}, u32[]{:S(2)}, u32[]{:S(2)}) async-start(bf16[24,16,128]{2,1,0:T(8,128)(2,1)} %broadcast_in_dim.68), calls=%async_computation | async-start | bytes 196608 | tf_op jit(solution)/shard_map/all_to_all | solution.py:345
  53.9 0.7 add_multiply_fusion
  54.6 0.9 fusion
  55.5 0.7 dynamic_slice.6
  56.2 0.7 compare_convert_fusion
  57.0 0.1 constant_dynamic-slice_fusion
  57.0 0.6 fusion.2
  57.7 0.6 fusion.3
  58.2 3.1 %select_select_fusion = (f32[16]{0:T(128)}, f32[16]{0:T(128)}) fusion(f32[]{:T(128)} %bitcast.3, pred[]{:T(512)S(6)} %eq.52, f32[]{:T(128)} %bitcast.2, f32[]{:T(128)} %bitcast.1, f32[]{:T(128)} %bitcast), kind=kLoop, calls=%fused_computation.22 | loop fusion | flops 528 | bytes 145 | tf_op jit(solution)/shard_map/jit(_where)/select_n | solution.py:390
  61.4 3.7 %all-to-all-done = bf16[24,16,128]{2,1,0:T(8,128)(2,1)} async-done(((bf16[24,16,128]{2,1,0:T(8,128)(2,1)}), bf16[24,16,128]{2,1,0:T(8,128)(2,1)}, u32[]{:S(2)}, u32[]{:S(2)}) %all-to-all-start) | async-done | bytes 98336 | tf_op jit(solution)/shard_map/all_to_all | solution.py:345
  65.0 2.3 %bonds.1.refs_4_ = bf16[6,128,384]{2,1,0:T(8,128)(2,1)} custom-call(bf16[384,128]{1,0:T(8,128)(2,1)} %bitcast.10.table_ref), custom_call_target="tpu_custom_call" | custom-call | flops 1000000 | bytes 1000000 | tf_op jit(solution)/shard_map/bonds/pallas_call | solution.py:204
  67.3 0.0 collective-permute-done.2.refs_2_
  67.3 0.0 copy-start
  67.3 0.0 collective-permute-done.3.refs_3_
  67.3 0.0 copy-start.1
  67.3 0.9 copy-done
  68.2 0.3 copy-done.1
  68.5 3.4 %traced.1 = f32[2,6,128]{2,1,0:T(8,128)} custom-call(f32[16]{0:T(128)} %get-tuple-element.14.refs_0_.c_ref, bf16[12,288,128]{2,1,0:T(8,128)(2,1)} %keldysh.2.refs_1_.refs_0_, bf16[12,288,128]{2,1,0:T(8,128)(2,1)} %keldysh.3.refs_1_, bf16[12,288,128]{2,1,0:T(8,128)(2,1)} %copy-done, bf16[12,288,128]{2,1,0:T(8,128)(2,1)} %copy-done.1), custom_call_target="tpu_custom_call" | custom-call | flops 3538944 | bytes 3538944 | tf_op jit(solution)/shard_map/traced/pallas_call | solution.py:330
  71.8 0.8 reshape.68
  72.6 0.7 reshape.69
  73.3 6.0 %all-to-all-start.1 = ((f32[24,1,64]{2,1,0:T(1,128)}), f32[24,1,64]{2,1,0:T(1,128)S(1)}, u32[]{:S(2)}, u32[]{:S(2)}) async-start(f32[24,1,64]{2,1,0:T(1,128)} %bitcast.20), calls=%async_computation.1 | async-start | bytes 24576 | tf_op jit(solution)/shard_map/all_to_all | solution.py:419
  79.3 4.3 %scattered.2.refs_5_ = bf16[2,2,1728,128]{3,2,1,0:T(8,128)(2,1)} custom-call(f32[16]{0:T(128)} %get-tuple-element.14.refs_0_.c_ref, bf16[12,288,128]{2,1,0:T(8,128)(2,1)} %keldysh.3.refs_1_, bf16[12,288,128]{2,1,0:T(8,128)(2,1)} %copy-done, bf16[12,288,128]{2,1,0:T(8,128)(2,1)} %copy-done.1, bf16[6,128,384]{2,1,0:T(8,128)(2,1)} %bonds.1.refs_4_), custom_call_target="tpu_custom_call" | custom-call | flops 339738624 | bytes 3538944 | tf_op jit(solution)/shard_map/scattered/pallas_call | solution.py:266
  83.7 5.1 %all-to-all-done.1 = f32[24,1,64]{2,1,0:T(1,128)S(1)} async-done(((f32[24,1,64]{2,1,0:T(1,128)}), f32[24,1,64]{2,1,0:T(1,128)S(1)}, u32[]{:S(2)}, u32[]{:S(2)}) %all-to-all-start.1) | async-done | bytes 6176 | tf_op jit(solution)/shard_map/all_to_all | solution.py:419
  88.8 0.6 broadcast_in_dim.69
  89.4 11.2 %all-to-all-start.2 = ((f32[32,1,64]{2,1,0:T(1,128)}), f32[32,1,64]{2,1,0:T(1,128)S(1)}, u32[]{:S(2)}, u32[]{:S(2)}) async-start(f32[32,1,64]{2,1,0:T(1,128)} %broadcast_in_dim.69), calls=%async_computation.2 | async-start | bytes 32768 | tf_op jit(solution)/shard_map/all_to_all | solution.py:345
  100.7 0.0 collective-permute-done.refs_2_
  100.7 0.0 copy-start.2
  100.7 0.0 collective-permute-done.1.refs_3_
  100.7 0.0 copy-start.3
  100.7 0.9 copy-done.2
  101.6 0.3 copy-done.3
  101.9 4.3 %scattered.3 = bf16[2,2,1728,128]{3,2,1,0:T(8,128)(2,1)} custom-call(f32[16]{0:T(128)} %get-tuple-element.15.refs_0_, bf16[12,288,128]{2,1,0:T(8,128)(2,1)} %keldysh.2.refs_1_.refs_0_, bf16[12,288,128]{2,1,0:T(8,128)(2,1)} %copy-done.2, bf16[12,288,128]{2,1,0:T(8,128)(2,1)} %copy-done.3, ...), custom_call_target="tpu_custom_call", output_to_operand_aliasing={{}: (5, {})} | custom-call | flops 339738624 | bytes 3538944 | tf_op jit(solution)/shard_map/scattered/pallas_call | solution.py:266
  106.3 2.8 %all-to-all-done.2 = f32[32,1,64]{2,1,0:T(1,128)S(1)} async-done(((f32[32,1,64]{2,1,0:T(1,128)}), f32[32,1,64]{2,1,0:T(1,128)S(1)}, u32[]{:S(2)}, u32[]{:S(2)}) %all-to-all-start.2) | async-done | bytes 8224 | tf_op jit(solution)/shard_map/all_to_all | solution.py:345
  109.2 0.1 slice_bitcast_fusion.2
  109.2 0.6 multiply_multiply_fusion
  (8 shorter events, 0.1 us)
Async XLA Ops:
  11.2 56.1 %collective-permute-start.2 = (bf16[12,288,128]{2,1,0:T(8,128)(2,1)}, bf16[12,288,128]{2,1,0:T(8,128)(2,1)S(1)}, u32[]{:S(2)}, u32[]{:S(2)}) collective-permute-start(bf16[12,288,128]{2,1,0:T(8,128)(2,1)} %keldysh.3.refs_1_), channel_id=1, source_target_pairs={{0,1},{1,0},{2,3},{3,2},{4,5},{5,4},{6,7},{7,6},{8,9},{9,8},{10,11... | collective-permute-start | bytes 2654216 | tf_op jit(solution)/shard_map/ppermute | solution.py:406
  23.5 43.8 %collective-permute-start.3 = (bf16[12,288,128]{2,1,0:T(8,128)(2,1)}, bf16[12,288,128]{2,1,0:T(8,128)(2,1)S(1)}, u32[]{:S(2)}, u32[]{:S(2)}) collective-permute-start(bf16[12,288,128]{2,1,0:T(8,128)(2,1)} %keldysh.3.refs_1_), channel_id=1, source_target_pairs={{1,2},{3,4},{5,6},{7,8},{9,10},{11,12},{13,14},{15,16},{17,18},{19... | collective-permute-start | bytes 2654216 | tf_op jit(solution)/shard_map/ppermute | solution.py:405
  36.0 64.7 %collective-permute-start = (bf16[12,288,128]{2,1,0:T(8,128)(2,1)}, bf16[12,288,128]{2,1,0:T(8,128)(2,1)S(1)}, u32[]{:S(2)}, u32[]{:S(2)}) collective-permute-start(bf16[12,288,128]{2,1,0:T(8,128)(2,1)} %keldysh.2.refs_1_.refs_0_), channel_id=1, source_target_pairs={{0,1},{1,0},{2,3},{3,2},{4,5},{5,4},{6,7},{7,6},{8,9},{9,8},{10,11... | collective-permute-start | bytes 2654216 | tf_op jit(solution)/shard_map/ppermute | solution.py:406
  37.9 62.8 %collective-permute-start.1 = (bf16[12,288,128]{2,1,0:T(8,128)(2,1)}, bf16[12,288,128]{2,1,0:T(8,128)(2,1)S(1)}, u32[]{:S(2)}, u32[]{:S(2)}) collective-permute-start(bf16[12,288,128]{2,1,0:T(8,128)(2,1)} %keldysh.2.refs_1_.refs_0_), channel_id=1, source_target_pairs={{1,2},{3,4},{5,6},{7,8},{9,10},{11,12},{13,14},{15,16},{17,18},{19... | collective-permute-start | bytes 2654216 | tf_op jit(solution)/shard_map/ppermute | solution.py:405
  46.3 18.7 %all-to-all-start = ((bf16[24,16,128]{2,1,0:T(8,128)(2,1)}), bf16[24,16,128]{2,1,0:T(8,128)(2,1)}, u32[]{:S(2)}, u32[]{:S(2)}) async-start(bf16[24,16,128]{2,1,0:T(8,128)(2,1)} %broadcast_in_dim.68), calls=%async_computation | async-start | bytes 196608 | tf_op jit(solution)/shard_map/all_to_all | solution.py:345
  67.3 0.9 copy-start
  67.3 1.2 %copy-start.1 = (bf16[12,288,128]{2,1,0:T(8,128)(2,1)}, bf16[12,288,128]{2,1,0:T(8,128)(2,1)S(1)}, u32[]{:S(2)}) copy-start(bf16[12,288,128]{2,1,0:T(8,128)(2,1)S(1)} %collective-permute-done.3.refs_3_) | copy-start | bytes 2654212
  73.3 15.5 %all-to-all-start.1 = ((f32[24,1,64]{2,1,0:T(1,128)}), f32[24,1,64]{2,1,0:T(1,128)S(1)}, u32[]{:S(2)}, u32[]{:S(2)}) async-start(f32[24,1,64]{2,1,0:T(1,128)} %bitcast.20), calls=%async_computation.1 | async-start | bytes 24576 | tf_op jit(solution)/shard_map/all_to_all | solution.py:419
  89.4 19.7 %all-to-all-start.2 = ((f32[32,1,64]{2,1,0:T(1,128)}), f32[32,1,64]{2,1,0:T(1,128)S(1)}, u32[]{:S(2)}, u32[]{:S(2)}) async-start(f32[32,1,64]{2,1,0:T(1,128)} %broadcast_in_dim.69), calls=%async_computation.2 | async-start | bytes 32768 | tf_op jit(solution)/shard_map/all_to_all | solution.py:345
  100.7 0.9 copy-start.2
  100.7 1.2 %copy-start.3 = (bf16[12,288,128]{2,1,0:T(8,128)(2,1)}, bf16[12,288,128]{2,1,0:T(8,128)(2,1)S(1)}, u32[]{:S(2)}) copy-start(bf16[12,288,128]{2,1,0:T(8,128)(2,1)S(1)} %collective-permute-done.1.refs_3_) | copy-start | bytes 2654212
